TPU v7x, 32 devices: a whole 2x2x4 slice. The times are simulated.
32 devices in a mesh: dp: 8 (over z, core), tp: 4 (over y, x).
Axes of the slice: x: 2, y: 2, z: 4, core: 2. Of those that a mesh axis runs over, the one named last changes fastest.
Arguments:
- x_in: bfloat16 [8192, 2048], P(('dp', 'tp')), may hold values from -6 to 6
- norm_gain: float32 [2048], replicated, may hold values from 0.5 to 1.5
- w_z: bfloat16 [2048, 4096], P(None, 'tp'), may hold values from -0.125 to 0.125
- w_x: bfloat16 [2048, 4096], P(None, 'tp'), may hold values from -0.125 to 0.125
- w_b: bfloat16 [2048, 128], P(None, 'tp'), may hold values from -0.125 to 0.125
- w_c: bfloat16 [2048, 128], P(None, 'tp'), may hold values from -0.125 to 0.125
- w_dt: bfloat16 [2048, 64], P(None, 'tp'), may hold values from -0.125 to 0.125
- conv_w: float32 [4352, 4], replicated, may hold values from -3 to 3
- conv_b: float32 [4352], replicated, may hold values from -3 to 3
- dt_bias: float32 [64], replicated, may hold values from -6 to -2
- a_log: float32 [64], replicated, may hold values from -2.5 to 0.5
- d_skip: float32 [64], replicated, may hold values from 0.5 to 1.5
- gate_gain: float32 [4096], replicated, may hold values from 0.5 to 1.5
- w_out: bfloat16 [4096, 2048], P('tp'), may hold values from -0.09375 to 0.09375
- doc_lens: int32 [8, 8], P('dp'), may hold values from 1 to 512, 1024 in all within a row
- d_out: bfloat16 [8192, 2048], P(('dp', 'tp')), may hold values from -6 to 6
Outputs:
- block_out: bfloat16 [8192, 2048], P(('dp', 'tp'))
- grad_x: float32 [8192, 2048], P(('dp', 'tp'))
- grad_norm_gain: float32 [2048], replicated
- grad_w_z: float32 [2048, 4096], P('dp', 'tp')
- grad_w_x: float32 [2048, 4096], P('dp', 'tp')
- grad_w_b: float32 [2048, 128], P('dp', 'tp')
- grad_w_c: float32 [2048, 128], P('dp', 'tp')
- grad_w_dt: float32 [2048, 64], P('dp', 'tp')
- grad_conv_w: float32 [4352, 4], replicated
- grad_conv_b: float32 [4352], replicated
- grad_dt_bias: float32 [64], replicated
- grad_a_log: float32 [64], replicated
- grad_d_skip: float32 [64], replicated
- grad_gate_gain: float32 [4096], replicated
- grad_w_out: float32 [4096, 2048], P('tp', 'dp')
Inputs may be any that keep to these rules, and one draw needn't show every extreme that they name: `doc_lens`: each row gives, in order, the lengths of the 8 documents packed into one sequence of 1024 tokens; a row sums to 1024 and its longest document has exactly 512 tokens.
All inputs are finite; a program needn't handle non-finite values.
Results may differ from a plain program's by a relative error of at most 0.012.
Values may be sent and summed in bfloat16 or wider, within the bound.
A program may use at most 256 MiB of HBM per device.

v0:
```python
import jax
import jax.numpy as jnp
from jax import lax
from jax.sharding import PartitionSpec as P

EPSILON = 1e-05
HIGHEST = lax.Precision.HIGHEST


def entering_2(array, axis, combine, identity, reverse):
    count, index = (lax.axis_size(axis), lax.axis_index(axis))
    everything = jax.tree.map(lambda part: lax.all_gather(part, axis), array)
    start = jax.tree.map(
        lambda part, zero: jnp.broadcast_to(jnp.asarray(zero, part.dtype), part.shape),
        array,
        identity,
    )

    def lap(k, before):
        at = count - 1 - k if reverse else k
        reached = at > index if reverse else at < index
        new = combine(before, jax.tree.map(lambda part: part[at], everything))
        return jax.tree.map(lambda a, b: jnp.where(reached, a, b), new, before)

    return lax.fori_loop(0, count, lap, start)


def span_parts(log_decay, segments, segment_prev):
    cumulative = jnp.cumsum(log_decay, axis=0)
    inward = jnp.exp(cumulative) * (segments == segment_prev).astype(jnp.float32)[:, None]
    carried = jnp.exp(cumulative[-1]) * (segments[-1] == segment_prev).astype(jnp.float32)
    return (cumulative, inward, carried)


def span_pass(state, values, b_rows, c_rows, log_decay, steps_dt, segments, segment_prev):
    cumulative, inward, carried = span_parts(log_decay, segments, segment_prev)
    length = segments.shape[0]
    order = jnp.arange(length, dtype=jnp.int32)
    same = (segments[:, None] == segments[None, :]) & (order[:, None] >= order[None, :])
    spread = cumulative[:, None, :] - cumulative[None, :, :]
    decays = jnp.exp(jnp.where(same[:, :, None], spread, -1e30))
    scores = jnp.dot(c_rows, b_rows.T, precision=HIGHEST)
    mixing = decays * scores[:, :, None] * steps_dt[None, :, :]
    output = jnp.einsum("tsh,shp->thp", mixing, values, precision=HIGHEST)
    output = (
        output + jnp.einsum("tn,hpn->thp", c_rows, state, precision=HIGHEST) * inward[:, :, None]
    )
    tail_same = segments == segments[-1]
    tail = (
        jnp.exp(jnp.where(tail_same[:, None], cumulative[-1][None, :] - cumulative, -1e30))
        * steps_dt
    )
    weighted = tail[:, :, None] * values
    state_out = carried[:, None, None] * state + jnp.einsum(
        "shp,sn->hpn", weighted, b_rows, precision=HIGHEST
    )
    return (output, state_out, carried)


def in_norm(values, gain):
    return (
        values
        * lax.rsqrt(jnp.mean(values * values, axis=-1, keepdims=True) + EPSILON)
        * gain[None, :]
    )


def combine(earlier, later):
    return (earlier[0] * later[0], later[0][:, None, None] * earlier[1] + later[1])


def body(
    x_in,
    norm_gain,
    w_z,
    w_x,
    w_b,
    w_c,
    w_dt,
    conv_w,
    conv_b,
    dt_bias,
    a_log,
    d_skip,
    gate_gain,
    w_out,
    doc_lens,
    d_out,
):
    tp_count = lax.axis_size("tp")
    tp_rank = lax.axis_index("tp")
    dev_rows = x_in.shape[0]
    group_rows = dev_rows * tp_count
    head_count = dt_bias.shape[0]
    inner_width = gate_gain.shape[0]
    head_size = inner_width // head_count
    state_size = (conv_w.shape[0] - inner_width) // 2
    rim_rows = conv_w.shape[1] - 1
    col_widths = [w_z.shape[1], w_x.shape[1], w_b.shape[1], w_c.shape[1], w_dt.shape[1]]
    col_edges = [0]
    for col_width in col_widths:
        col_edges.append(col_edges[-1] + col_width)
    total_cols = col_edges[-1]
    contract_first = (((0,), (0,)), ((), ()))
    contract_last = (((1,), (1,)), ((), ()))
    lengths = doc_lens[0]
    doc_starts = jnp.cumsum(lengths) - lengths
    positions = tp_rank * dev_rows - rim_rows + jnp.arange(dev_rows + rim_rows, dtype=jnp.int32)
    seg_ext = jnp.sum((positions[:, None] >= doc_starts[None, :]).astype(jnp.int32), axis=1)
    seg_own = seg_ext[rim_rows:]
    seg_before = [seg_ext[rim_rows - 1]]
    x_float = x_in.astype(jnp.float32)
    normed = in_norm(x_float, norm_gain).astype(jnp.bfloat16)
    w_joined = jnp.concatenate([w_z, w_x, w_b, w_c, w_dt], axis=1)
    gathered = lax.all_gather(normed, "tp", axis=0, tiled=True)
    projected = jnp.dot(gathered, w_joined, preferred_element_type=jnp.float32).astype(jnp.bfloat16)
    padded = jnp.concatenate([jnp.zeros((rim_rows, total_cols), jnp.bfloat16), projected], axis=0)
    rims = padded[:group_rows].reshape(tp_count, dev_rows, total_cols)[:, :rim_rows]
    blocks = jnp.concatenate([rims, projected.reshape(tp_count, dev_rows, total_cols)], axis=1)
    arrived = lax.all_to_all(blocks, "tp", split_axis=0, concat_axis=2, tiled=True).reshape(
        dev_rows + rim_rows, tp_count, total_cols
    )

    def columns(source, which):
        return source[:, :, col_edges[which] : col_edges[which + 1]].reshape(source.shape[0], -1)

    gate_in = columns(arrived[rim_rows:], 0).astype(jnp.float32)
    conv_in = jnp.concatenate(
        [columns(arrived, 1), columns(arrived, 2), columns(arrived, 3)], axis=1
    ).astype(jnp.float32)
    dt_in = columns(arrived[rim_rows:], 4).astype(jnp.float32)

    def prepare(conv_in, dt_in, conv_w, conv_b, dt_bias, a_log):
        summed = jnp.zeros((dev_rows, conv_in.shape[1]), jnp.float32) + conv_b[None, :]
        for kernel_tap in range(conv_w.shape[1]):
            match = (seg_ext[kernel_tap : kernel_tap + dev_rows] == seg_own).astype(jnp.float32)
            summed = (
                summed
                + conv_w[:, kernel_tap][None, :]
                * conv_in[kernel_tap : kernel_tap + dev_rows]
                * match[:, None]
            )
        active = jax.nn.silu(summed)
        values = active[:, :inner_width].reshape(dev_rows, head_count, head_size)
        b_rows = active[:, inner_width : inner_width + state_size]
        c_rows = active[:, inner_width + state_size :]
        steps_dt = jax.nn.softplus(dt_in + dt_bias[None, :])
        log_decay = -steps_dt * jnp.exp(a_log)[None, :]
        return (values, b_rows, c_rows, log_decay, steps_dt)

    prepared, prepare_back = jax.vjp(prepare, conv_in, dt_in, conv_w, conv_b, dt_bias, a_log)
    values, b_rows, c_rows, log_decay, steps_dt = prepared

    def ssd_local(values, b_rows, c_rows, log_decay, steps_dt):
        state = jnp.zeros((head_count, head_size, state_size), jnp.float32)
        carried_all = jnp.ones((head_count,), jnp.float32)
        output, state, carried = span_pass(
            state, values, b_rows, c_rows, log_decay, steps_dt, seg_own, seg_before[0]
        )
        outputs = [output]
        carried_all = carried_all * carried
        return (jnp.concatenate(outputs, axis=0), carried_all, state)

    def entering(state_in, c_rows, log_decay):
        decay = jnp.ones((head_count,), jnp.float32)
        cumulative, inward, carried = span_parts(log_decay, seg_own, seg_before[0])
        reached = jnp.einsum(
            "tn,hpn->thp", c_rows, decay[:, None, None] * state_in, precision=HIGHEST
        )
        outputs = [reached * inward[:, :, None]]
        return jnp.concatenate(outputs, axis=0)

    identity = (
        jnp.ones((head_count,), jnp.float32),
        jnp.zeros((head_count, head_size, state_size), jnp.float32),
    )
    local_parts, ssd_back = jax.vjp(ssd_local, values, b_rows, c_rows, log_decay, steps_dt)
    local_out, carried_dev, state_dev = local_parts
    chained = entering_2((carried_dev, state_dev), "tp", combine, identity, False)
    state_in = chained[1]
    extra_out, entering_back = jax.vjp(entering, state_in, c_rows, log_decay)
    ssd_out = local_out + extra_out

    def gated(ssd_out, values, gate_in, d_skip, gate_gain):
        mixed_heads = ssd_out + d_skip[None, :, None] * values
        flat = mixed_heads.reshape(dev_rows, inner_width)
        gated_rows = flat * jax.nn.silu(gate_in)
        scale = lax.rsqrt(jnp.mean(gated_rows * gated_rows, axis=-1, keepdims=True) + EPSILON)
        return gated_rows * scale * gate_gain[None, :]

    normal_out, gated_back = jax.vjp(gated, ssd_out, values, gate_in, d_skip, gate_gain)
    rounded = normal_out.astype(jnp.bfloat16)
    by_heads = lax.all_to_all(rounded, "tp", split_axis=1, concat_axis=0, tiled=True)
    branch_out = lax.psum_scatter(
        jnp.dot(by_heads, w_out, preferred_element_type=jnp.float32),
        "tp",
        scatter_dimension=0,
        tiled=True,
    )
    block_out = (x_float + branch_out).astype(jnp.bfloat16)
    grad_gathered = lax.all_gather(d_out, "tp", axis=0, tiled=True)
    grad_heads = lax.dot_general(
        grad_gathered, w_out, contract_last, preferred_element_type=jnp.float32
    ).astype(jnp.bfloat16)
    grad_normal = lax.all_to_all(grad_heads, "tp", split_axis=0, concat_axis=1, tiled=True)
    grad_ssd, grad_values_a, grad_gate_in, grad_skip, grad_gate_gain = gated_back(
        grad_normal.astype(jnp.float32)
    )
    grad_state_in, grad_c_a, grad_decay_a = entering_back(grad_ssd)
    chained_back = entering_2((carried_dev, grad_state_in), "tp", combine, identity, True)
    grad_state_dev = chained_back[1]
    grad_carried = jnp.sum(grad_state_dev * state_in, axis=(1, 2))
    grad_values_b, grad_b, grad_c_b, grad_decay_b, grad_dt = ssd_back(
        (grad_ssd, grad_carried, grad_state_dev)
    )
    grad_conv_in, grad_dt_in, grad_conv_w, grad_conv_b, grad_dt_bias, grad_a_log = prepare_back(
        (
            grad_values_a + grad_values_b,
            grad_b,
            grad_c_a + grad_c_b,
            grad_decay_a + grad_decay_b,
            grad_dt,
        )
    )

    def split_heads(array):
        return array.reshape(array.shape[0], tp_count, -1)

    grad_gate_full = jnp.concatenate(
        [jnp.zeros((rim_rows, inner_width), jnp.float32), grad_gate_in], axis=0
    )
    grad_dt_full = jnp.concatenate(
        [jnp.zeros((rim_rows, head_count), jnp.float32), grad_dt_in], axis=0
    )
    pieces = [
        split_heads(grad_gate_full),
        split_heads(grad_conv_in[:, :inner_width]),
        split_heads(grad_conv_in[:, inner_width : inner_width + state_size]),
        split_heads(grad_conv_in[:, inner_width + state_size :]),
        split_heads(grad_dt_full),
    ]
    outgoing = jnp.concatenate(pieces, axis=2).reshape(
        1, dev_rows + rim_rows, tp_count * total_cols
    )
    returned = lax.all_to_all(outgoing, "tp", split_axis=2, concat_axis=0, tiled=True)
    main_rows = returned[:, rim_rows:]
    main_rows = main_rows.at[:-1, dev_rows - rim_rows :].add(returned[1:, :rim_rows])
    grad_projected = main_rows.reshape(group_rows, total_cols).astype(jnp.bfloat16)
    grad_normed = lax.psum_scatter(
        lax.dot_general(
            grad_projected, w_joined, contract_last, preferred_element_type=jnp.float32
        ),
        "tp",
        scatter_dimension=0,
        tiled=True,
    )
    _, norm_back = jax.vjp(in_norm, x_float, norm_gain)
    grad_x_norm, grad_norm_gain = norm_back(grad_normed)
    grad_x = d_out.astype(jnp.float32) + grad_x_norm
    in_part = lax.dot_general(
        gathered, grad_projected, contract_first, preferred_element_type=jnp.float32
    )
    weight_grads = lax.psum_scatter(
        jnp.concatenate(
            [
                in_part,
                lax.dot_general(
                    grad_gathered, by_heads, contract_first, preferred_element_type=jnp.float32
                ),
            ],
            axis=1,
        ),
        "dp",
        scatter_dimension=0,
        tiled=True,
    )
    grad_w_z = weight_grads[:, col_edges[0] : col_edges[1]]
    grad_w_x = weight_grads[:, col_edges[1] : col_edges[2]]
    grad_w_b = weight_grads[:, col_edges[2] : col_edges[3]]
    grad_w_c = weight_grads[:, col_edges[3] : col_edges[4]]
    grad_w_dt = weight_grads[:, col_edges[4] : col_edges[5]]
    grad_w_out = weight_grads[:, total_cols:].T
    summed_small = lax.psum(
        (
            grad_norm_gain,
            grad_conv_w,
            grad_conv_b,
            grad_dt_bias,
            grad_a_log,
            grad_skip,
            grad_gate_gain,
        ),
        ("dp", "tp"),
    )
    return (
        block_out,
        grad_x,
        summed_small[0],
        grad_w_z,
        grad_w_x,
        grad_w_b,
        grad_w_c,
        grad_w_dt,
        summed_small[1],
        summed_small[2],
        summed_small[3],
        summed_small[4],
        summed_small[5],
        summed_small[6],
        grad_w_out,
    )


def solution(mesh):
    placed = (
        P(("dp", "tp"), None),
        P(),
        P(None, "tp"),
        P(None, "tp"),
        P(None, "tp"),
        P(None, "tp"),
        P(None, "tp"),
        P(),
        P(),
        P(),
        P(),
        P(),
        P(),
        P("tp", None),
        P("dp", None),
        P(("dp", "tp"), None),
    )
    return jax.shard_map(
        body,
        mesh=mesh,
        in_specs=placed,
        out_specs=(
            P(("dp", "tp"), None),
            P(("dp", "tp"), None),
            P(),
            P("dp", "tp"),
            P("dp", "tp"),
            P("dp", "tp"),
            P("dp", "tp"),
            P("dp", "tp"),
            P(),
            P(),
            P(),
            P(),
            P(),
            P(),
            P("tp", "dp"),
        ),
        check_vma=False,
    )
```

profile of v0, /device:TPU:1, one launch (start us, length us, event | category | flops | bytes accessed | tf_op | source)
XLA Modules:
  0.0 1443.4 jit_solution(17318158812077434221)
XLA Ops:
  12.3 14.3 concatenate.29
  26.6 39.8 %all-gather.8.cloned.1.call-done = bf16[1024,2048]{1,0:T(8,128)(2,1)} async-done(((bf16[256,2048]{1,0:T(8,128)(2,1)}), bf16[1024,2048]{1,0:T(8,128)(2,1)}) %all-gather.8.cloned.1.call-update) | async-done | bytes 4194320 | tf_op jit(solution)/shard_map/all_gather | solution.py:115
  66.3 13.6 convolution_convert_fusion
  82.0 4.6 pad_slice_fusion
  86.6 6.4 copy.204
  93.1 6.4 copy.203
  100.4 5.6 pad_maximum_fusion.1
  106.0 5.0 all-to-all-start
  117.4 60.6 %all-to-all-done = bf16[4,259,2128]{2,1,0:T(8,128)(2,1)} async-done(((bf16[4,259,2128]{2,1,0:T(8,128)(2,1)}), bf16[4,259,2128]{2,1,0:T(8,128)(2,1)}, u32[]{:S(2)}, u32[]{:S(2)}) %all-to-all-start) | async-done | bytes 4409248 | tf_op jit(solution)/shard_map/all_to_all | solution.py:120
  178.0 8.2 copy.176
  186.2 5.1 slice_bitcast_fusion
  202.5 4.9 fusion.25
  212.1 5.8 copy.180
  218.3 7.0 fusion.78
  225.4 8.0 convolution_convert_fusion.1
  236.0 4.5 all-to-all-start.2
  240.8 43.3 %all-to-all-done.2 = bf16[4,256,1024]{1,2,0:T(8,128)(2,1)} async-done(((bf16[4,256,1024]{1,2,0:T(8,128)(2,1)}), bf16[4,256,1024]{1,2,0:T(8,128)(2,1)}, u32[]{:S(2)}, u32[]{:S(2)}) %all-to-all-start.2) | async-done | bytes 2097184 | tf_op jit(solution)/shard_map/all_to_all | solution.py:205
  284.1 4.0 convert_element_type.132
  288.1 6.3 all-gather.2
  295.7 6.2 fusion.92
  305.8 32.7 %all-gather.12.cloned.1.call-done = f32[256,64,128]{2,1,0:T(8,128)} async-done(((f32[64,64,128]{2,1,0:T(8,128)}), f32[256,64,128]{2,1,0:T(8,128)}) %all-gather.12.cloned.1.call-update) | async-done | bytes 8388624 | tf_op jit(solution)/shard_map/all_gather | solution.py:12
  338.5 8.5 while.31
  347.0 4.5 fusion.100
  351.5 23.6 %multiply_reduce_fusion.11 = (f32[256]{0:T(256)S(1)}, f32[256,64,64]{0,2,1:T(8,128)S(1)}, f32[256,64,64]{0,2,1:T(8,128)}) fusion(f32[256,64,64]{0,2,1:T(8,128)} %bitcast.311, f32[256,64,64]{0,2,1:T(8,128)S(1)} %bitcast.299, f32[64]{0:T(128)S(1)} %copy-done.73, f32[256,64,64]{0,2,1:T(8,128)S(1)} %fusion.100, f32[256,64,64]{0,2,1:T(8,128)} %fusion.92, ...), kind=kOutput, calls=%fused_computation.87 | convolution fusion | flops 3251633920 | bytes 25691392 | tf_op jit(solution)/shard_map/jvp(tsh,shp->thp)/dot_general | solution.py:44
  377.4 6.0 multiply_reduce_fusion.6
  385.3 5.6 fusion.53
  393.7 5.0 fusion.28
  398.7 4.7 concatenate.33
  403.4 7.6 copy.193
  411.0 8.8 fusion.84
  419.8 6.7 fusion.81
  426.6 26.2 %fusion.10 = (f32[256,64]{0,1:T(8,128)S(1)}, f32[256,64]{0,1:T(8,128)S(1)}, f32[256,64]{0,1:T(8,128)}, f32[256,256]{1,0:T(8,128)S(1)}) fusion(f32[256,64]{0,1:T(8,128)S(1)} %copy-done.43, f32[256,256]{1,0:T(8,128)S(1)} %copy-done.23, f32[256,64]{0,1:T(8,128)S(1)} %bitcast_bitcast_fusion.1, pred[256,256]{1,0:T(8,128)(4,1)S(1)} %fusion.95, ...), kind=kOutput, calls=%fused_computation.18 | convolution fusion | flops 3275636736 | bytes 9306112 | tf_op jit(solution)/shard_map/transpose(jvp(tsh,shp->thp))/dot_general | solution.py:44
  454.0 24.7 %all-gather.14.cloned.1.call-done = f32[256,64,128]{2,1,0:T(8,128)} async-done(((f32[64,64,128]{2,1,0:T(8,128)}), f32[256,64,128]{2,1,0:T(8,128)}) %all-gather.14.cloned.1.call-update) | async-done | bytes 8388624 | tf_op jit(solution)/shard_map/all_gather | solution.py:12
  478.7 14.9 %while.32 = (s32[]{:T(128)}, f32[64,64,128]{2,1,0:T(8,128)}, s32[]{:T(128)}, f32[4,64]{1,0:T(4,128)S(1)}, f32[4,64,64,128]{3,2,1,0:T(8,128)}, /*index=5*/s32[]{:T(128)}, s32[]{:T(128)}, s32[]{:T(128)}, s32[]{:T(128)}) while((s32[]{:T(128)}, f32[64,64,128]{2,1,0:T(8,128)}, s32[]{:T(128)}, f32[4,64]{1,0:T(4,128)S(1)}, ...), condition=%wide.region_12.13_spmd.clone, body=%wide.region_11.12_spmd.clone.sunk | while | flops 2097160 | bytes 6292391 | solution.py:25
  493.6 9.8 fusion.87
  503.5 4.5 multiply_reduce_fusion.9
  510.5 15.7 %fusion.31 = f32[256,64,64]{0,2,1:T(8,128)} fusion(f32[256,64,64]{0,2,1:T(8,128)S(1)} %get-tuple-element.469, f32[256,64,64]{0,2,1:T(8,128)S(1)} %copy-done.7, f32[64]{0:T(128)S(1)} %copy-done.73, f32[256,64]{0,1:T(8,128)S(1)} %get-tuple-element.456, f32[256,64]{0,1:T(8,128)S(1)} %copy-done.43, f32[256,256]{1,0:T(8,128)S(1)} %copy-done.24, ...), kind=kOutput, calls=%fused_computation.58 | convolution fusion | flops 3242196992 | bytes 13107456 | tf_op jit(solution)/shard_map/transpose(jvp(tsh,shp->thp))/dot_general | solution.py:44
  526.2 6.0 copy.185
  532.2 12.2 multiply_reduce_fusion.4
  549.5 7.2 pad_add_fusion
  561.6 4.7 slice.230
  566.3 6.1 reshape.445
  572.4 15.8 %concatenate.35 = f32[259,4,2128]{2,1,0:T(4,128)} concatenate(f32[259,4,1024]{2,1,0:T(4,128)} %copy.193, f32[259,4,1024]{2,1,0:T(4,128)} %reshape.445, f32[259,4,32]{2,1,0:T(4,128)S(1)} %copy.194, f32[259,4,32]{2,1,0:T(4,128)S(1)} %copy.195, f32[259,4,16]{2,1,0:T(4,128)S(1)} %copy.196), dimensions={2} | concatenate | bytes 17636864 | tf_op jit(solution)/shard_map/concatenate | solution.py:242
  588.2 11.4 reshape.454
  599.6 27.3 %copy.197 = f32[1,259,8512]{1,0,2:T(1,128)} copy(f32[1,259,8512]{2,1,0:T(8,128)} %reshape.454) | data formatting | bytes 17636864 | tf_op jit(solution)/shard_map/reshape | solution.py:242
  626.8 6.5 all-to-all-start.3
  634.7 140.7 %all-to-all-done.3 = f32[1,259,8512]{1,0,2:T(1,128)} async-done(((f32[1,259,8512]{1,0,2:T(1,128)}), f32[1,259,8512]{1,0,2:T(1,128)}, u32[]{:S(2)}, u32[]{:S(2)}) %all-to-all-start.3) | async-done | bytes 8818464 | tf_op jit(solution)/shard_map/all_to_all | solution.py:245
  775.4 11.9 copy.207
  787.3 7.0 slice.233
  797.7 4.8 add_select_fusion
  802.5 22.9 %scatter-add.4 = f32[4,256,2128]{1,2,0:T(8,128)} dynamic-update-slice(f32[4,256,2128]{1,2,0:T(8,128)} %copy-done.8, f32[3,3,2128]{1,2,0:T(8,128)S(1)} %add_select_fusion, s32[]{:T(128)} %bitcast.52, s32[]{:T(128)} %bitcast.53, s32[]{:T(128)} %constant.140.clone.1) | dynamic-update-slice | bytes 153220 | tf_op jit(solution)/shard_map/scatter-add | solution.py:247
  825.4 5.9 convert_element_type.125
  831.3 6.4 copy.200
  837.7 15.7 %fusion.148 = f32[1024,2048]{1,0:T(8,128)} fusion(bf16[1024,2128]{1,0:T(8,128)(2,1)} %bitcast.319, bf16[2048,2128]{1,0:T(8,128)(2,1)} %concatenate.29), kind=kOutput, calls=%fused_computation.237 | convolution fusion | flops 8925478912 | bytes 21463040 | tf_op jit(solution)/shard_map/dot_general | solution.py:250
  857.8 49.7 %all_to_all.62 = bf16[256,4,1024]{0,2,1:T(8,128)(2,1)S(1)} all-to-all(bf16[256,4,1024]{0,2,1:T(8,128)(2,1)S(1)} %fusion.48), channel_id=1, replica_groups=mesh['dp'=8,'tp'=4] {'tp'}, dimensions={1} | all-to-all | bytes 4194304 | tf_op jit(solution)/shard_map/all_to_all | solution.py:193
  909.9 10.7 fusion.147
  922.2 9.1 convolution_bitcast_fusion
  931.3 12.9 fusion.149
  944.2 16.0 %pad_maximum_fusion = f32[2048,3152]{0,1:T(8,128)} fusion(f32[2048,1024]{0,1:T(8,128)} %convolution_bitcast_fusion, f32[2048,2128]{0,1:T(8,128)S(1)} %fusion.149), kind=kLoop, calls=%fused_computation.6 | loop fusion | flops 6455296 | bytes 51642368 | tf_op jit(solution)/shard_map/concatenate | solution.py:264
  965.7 41.9 %all-reduce.16 = (f32[2048]{0:T(1024)}, f32[4352]{0:T(1024)}, f32[64]{0:T(128)}, f32[64]{0:T(128)}, f32[64]{0:T(128)}, /*index=5*/f32[4096]{0:T(1024)}) all-reduce(f32[2048]{0:T(1024)S(1)} %get-tuple-element.395, f32[4352]{0:T(1024)S(1)} %copy-done.32, f32[64]{0:T(128)S(1)} %get-tuple-element.431, ...), channel_id=1, replica_groups=mesh['dp'=8,'tp'=4] {'dp','tp'}, use_global_device_ids=true, to_apply=%region_30.31 | all-reduce | flops 10688 | bytes 85504 | tf_op jit(solution)/shard_map/psum | solution.py:283
  1007.6 46.4 %reduce-scatter.4.cloned.1.call-done = f32[256,2048]{1,0:T(8,128)} async-done(((f32[1024,2048]{1,0:T(8,128)}), f32[256,2048]{1,0:T(8,128)}) %reduce-scatter.4.cloned.1.call-update) | async-done | bytes 2097168 | tf_op jit(solution)/shard_map/reduce_scatter | solution.py:194
  1054.0 4.3 fusion.65
  1058.3 249.3 %reduce-scatter.8.cloned.1.call-done = f32[256,3152]{0,1:T(8,128)} async-done(((f32[2048,3152]{0,1:T(8,128)}), f32[256,3152]{0,1:T(8,128)}) %reduce-scatter.8.cloned.1.call-update) | async-done | bytes 3227664 | tf_op jit(solution)/shard_map/reduce_scatter | solution.py:263
  1316.0 118.6 %all-reduce.19.cloned.1.call-done = f32[4352,4]{0,1:T(4,128)} async-done(((f32[4352,4]{0,1:T(4,128)}), f32[4352,4]{0,1:T(4,128)}) %all-reduce.19.cloned.1.call-update) | async-done | bytes 69648 | tf_op jit(solution)/shard_map/psum | solution.py:283
  (277 shorter events, 109.3 us)
Async XLA Ops:
  7.2 4.2 copy-start.30
  7.2 4.5 copy-start.31
  7.2 4.8 copy-start.39
  7.2 59.1 %all-gather.8.cloned.1.call-start = ((), (), s32[]{:S(2)}) async-start(), calls=%async_computation.7 | async-start | bytes 5242880 | tf_op jit(solution)/shard_map/all_gather | solution.py:115
  8.8 2.6 copy-start.66
  8.9 2.6 copy-start.57
  106.0 6.4 copy-start.74
  106.0 6.4 copy-start.72
  106.0 8.6 copy-start.38
  106.0 72.0 %all-to-all-start = ((bf16[4,259,2128]{2,1,0:T(8,128)(2,1)}), bf16[4,259,2128]{2,1,0:T(8,128)(2,1)}, u32[]{:S(2)}, u32[]{:S(2)}) async-start(bf16[4,259,2128]{2,1,0:T(8,128)(2,1)} %pad_maximum_fusion.1), calls=%async_computation | async-start | bytes 9191424 | tf_op jit(solution)/shard_map/all_to_all | solution.py:120
  111.1 114.3 %all-gather.10.cloned.1.call-start = ((), (), s32[]{:S(2)}) async-start(), calls=%async_computation.9 | async-start | bytes 5242880 | tf_op jit(solution)/shard_map/all_gather | solution.py:201
  111.8 226.7 %all-gather.12.cloned.1.call-start = ((), (), s32[]{:S(2)}) async-start(), calls=%async_computation.13 | async-start | bytes 10485760 | tf_op jit(solution)/shard_map/all_gather | solution.py:12
  112.4 80.9 %copy-start.68 = (f32[64]{0:T(128)}, f32[64]{0:T(128)S(1)}, u32[]{:S(2)}) copy-start(f32[64]{0:T(128)S(1)} %exp.58) | copy-start | bytes 772
  112.7 73.5 %copy-start.45 = (s32[259]{0:T(512)}, s32[259]{0:T(512)S(1)}, u32[]{:S(2)}) copy-start(s32[259]{0:T(512)S(1)} %convert_reduce_fusion) | copy-start | bytes 3112
  186.2 7.2 copy-start.59
  193.4 24.8 %copy-start.20 = (bf16[256,4,16]{0,2,1:T(8,128)(2,1)}, bf16[256,4,16]{0,2,1:T(8,128)(2,1)S(1)}, u32[]{:S(2)}) copy-start(bf16[256,4,16]{0,2,1:T(8,128)(2,1)S(1)} %slice.224) | copy-start | bytes 98308
  202.5 4.9 copy-start
  212.0 6.1 copy-start.50
  212.0 6.1 copy-start.60
  212.0 6.1 copy-start.64
  218.1 7.2 copy-start.62
  218.3 133.2 %copy-start.42 = (f32[256,64]{0,1:T(8,128)}, f32[256,64]{0,1:T(8,128)S(1)}, u32[]{:S(2)}) copy-start(f32[256,64]{0,1:T(8,128)S(1)} %get-tuple-element.457) | copy-start | bytes 196612
  233.4 7.2 copy-start.46
  233.4 7.2 copy-start.27
  236.0 48.2 %all-to-all-start.2 = ((bf16[4,256,1024]{1,2,0:T(8,128)(2,1)}), bf16[4,256,1024]{1,2,0:T(8,128)(2,1)}, u32[]{:S(2)}, u32[]{:S(2)}) async-start(bf16[4,256,1024]{1,2,0:T(8,128)(2,1)} %copy.184), calls=%async_computation.3 | async-start | bytes 4194304 | tf_op jit(solution)/shard_map/all_to_all | solution.py:205
  240.5 238.3 %all-gather.14.cloned.1.call-start = ((), (), s32[]{:S(2)}) async-start(), calls=%async_computation.14 | async-start | bytes 10485760 | tf_op jit(solution)/shard_map/all_gather | solution.py:12
  240.8 185.7 %copy-start.40 = (pred[256,256]{1,0:T(8,128)(4,1)}, pred[256,256]{1,0:T(8,128)(4,1)S(1)}, u32[]{:S(2)}) copy-start(pred[256,256]{1,0:T(8,128)(4,1)S(1)} %fusion.95) | copy-start | bytes 196612
  295.7 55.8 %copy-start.22 = (f32[256,256]{1,0:T(8,128)}, f32[256,256]{1,0:T(8,128)S(1)}, u32[]{:S(2)}) copy-start(f32[256,256]{1,0:T(8,128)S(1)} %fusion.106) | copy-start | bytes 786436
  347.0 4.5 copy-start.2
  347.0 4.5 copy-start.73
  351.5 23.7 %copy-start.16 = (f32[256,64,64]{0,2,1:T(8,128)}, f32[256,64,64]{0,2,1:T(8,128)S(1)}, u32[]{:S(2)}) copy-start(f32[256,64,64]{0,2,1:T(8,128)S(1)} %fusion.100) | copy-start | bytes 12582916
  351.5 23.6 %copy-start.11 = (f32[4,256,1024]{1,2,0:T(8,128)S(1)}, f32[4,256,1024]{1,2,0:T(8,128)}, u32[]{:S(2)}) copy-start(f32[4,256,1024]{1,2,0:T(8,128)} %convert_element_type.132) | copy-start | bytes 12582916
  375.1 18.6 %copy-start.47 = (f32[256]{0:T(256)}, f32[256]{0:T(256)S(1)}, u32[]{:S(2)}) copy-start(f32[256]{0:T(256)S(1)} %fusion.132) | copy-start | bytes 3076
  411.0 8.8 copy-start.6
  419.8 6.7 copy-start.3
  419.8 6.7 copy-start.23
  419.8 6.7 copy-start.43
  493.6 9.9 copy-start.1
  493.6 9.9 copy-start.4
  508.0 2.5 copy-start.7
  526.2 6.0 copy-start.52
  526.2 6.0 copy-start.54
  526.2 6.0 copy-start.56
  545.8 3.4 copy-start.10
  549.4 7.2 copy-start.21
  549.4 7.2 copy-start.61
  549.4 7.2 copy-start.63
  549.4 7.2 copy-start.65
  549.4 10.6 copy-start.44
  549.5 10.6 copy-start.69
  626.8 7.1 copy-start.71
  626.8 148.5 %all-to-all-start.3 = ((f32[1,259,8512]{1,0,2:T(1,128)}), f32[1,259,8512]{1,0,2:T(1,128)}, u32[]{:S(2)}, u32[]{:S(2)}) async-start(f32[1,259,8512]{1,0,2:T(1,128)} %copy.197), calls=%async_computation.4 | async-start | bytes 26148864 | tf_op jit(solution)/shard_map/all_to_all | solution.py:245
  633.3 329.9 %reduce-scatter.6.cloned.1.call-start = ((), (), s32[]{:S(2)}) async-start(), calls=%async_computation.10 | async-start | bytes 10485760 | tf_op jit(solution)/shard_map/reduce_scatter | solution.py:249
  794.3 3.4 copy-start.8
  853.5 200.5 %reduce-scatter.4.cloned.1.call-start = ((), (), s32[]{:S(2)}) async-start(), calls=%async_computation.8 | async-start | bytes 10485760 | tf_op jit(solution)/shard_map/reduce_scatter | solution.py:194
  920.6 387.0 %reduce-scatter.8.cloned.1.call-start = ((), (), s32[]{:S(2)}) async-start(), calls=%async_computation.11 | async-start | bytes 29048832 | tf_op jit(solution)/shard_map/reduce_scatter | solution.py:263
  960.2 3.0 copy-start.17
  960.3 3.0 copy-start.37
  960.3 3.0 copy-start.58
  960.3 5.4 copy-start.67
  960.3 5.4 copy-start.32
  960.3 5.4 copy-start.70
  960.3 474.2 %all-reduce.19.cloned.1.call-start = ((), (), s32[]{:S(2)}) async-start(), calls=%async_computation.12 | async-start | bytes 139264 | tf_op jit(solution)/shard_map/psum | solution.py:283
  963.3 90.7 %copy-start.18 = (f32[256,2048]{1,0:T(8,128)S(1)}, f32[256,2048]{1,0:T(8,128)}, u32[]{:S(2)}) copy-start(f32[256,2048]{1,0:T(8,128)} %reduce-scatter.6.cloned.1.call-done) | copy-start | bytes 6291460
  (23 other events, 38.0 us)
Sparse Core Ops, SparseCore 0:
  11.5 54.7 all-gather.7
  113.7 83.3 all-gather.9
  225.4 113.0 all-gather.11
  391.1 87.6 all-gather.13
  853.6 109.6 reduce-scatter.5
  966.5 87.4 reduce-scatter.3
  1056.3 251.1 reduce-scatter.7
  1314.7 119.8 all-reduce.18
where the time goes:
time: 1460 us; the launch traced here: 1440 us
  waiting for transfers between devices  758 us (52%)
  local copies, waits for them, and re-layouts  230 us (16%)
  matrix products  193 us (13%)
  other arithmetic  130 us (9%)
  blocking collectives  97.8 us (7%)
  between operations  17.1 us (1%)
  starting transfers between devices  16.9 us (1%)
    reduce_scatter x1, waiting for transfers between devices, body(): lax.psum_scatter(jnp.concatenate([in_part, lax.dot_general(grad_gathered,...  249 us
    all_to_all x1, waiting for transfers between devices, body(): lax.all_to_all(outgoing, 'tp', split_axis=2, concat_axis=0, tiled=True)  141 us
    psum x1, waiting for transfers between devices, body(): lax.psum((grad_norm_gain, grad_conv_w, grad_conv_b, grad_dt_bias, grad_a_...  119 us
    dot_general x3, matrix products, span_pass(): output = jnp.einsum('tsh,shp->thp', mixing, values, precision=HIGHEST)  65.4 us
    all_to_all x1, waiting for transfers between devices, body(): lax.all_to_all(blocks, 'tp', split_axis=0, concat_axis=2, tiled=True)  60.6 us
    all_gather x2, waiting for transfers between devices, entering_2(): everything = jax.tree.map(lambda part: lax.all_gather(part, axis), array)  57.4 us
    all_to_all x1, blocking collectives, body(): lax.all_to_all(rounded, 'tp', split_axis=1, concat_axis=0, tiled=True)  49.7 us
    reduce_scatter x1, waiting for transfers between devices, body(): lax.psum_scatter(jnp.dot(by_heads, w_out, preferred_element_type=jnp.floa...  46.4 us
  transfers between devices with their start and end apart: 11, of which 10 were waited for; matrix products, arithmetic and copies ran while one was open for 15% of the time, Pallas kernels for 0%

commit v1 on v0

--- a/solution.py
+++ b/solution.py
@@ -280,7 +280,7 @@
     grad_w_c = weight_grads[:, col_edges[3] : col_edges[4]]
     grad_w_dt = weight_grads[:, col_edges[4] : col_edges[5]]
     grad_w_out = weight_grads[:, total_cols:].T
-    summed_small = lax.psum(
+    partial = lax.psum(
         (
             grad_norm_gain,
             grad_conv_w,
@@ -290,8 +290,9 @@
             grad_skip,
             grad_gate_gain,
         ),
-        ("dp", "tp"),
-    )
+        "tp",
+    )
+    summed_small = lax.psum(partial, "dp")
     return (
         block_out,
         grad_x,

time: 1460 us -> 1390 us (0.952)
  waiting for transfers between devices: 758 us -> 688 us
    psum x1, waiting for transfers between devices: 119 us -> 0.02 us  [body(): lax.psum((grad_norm_gain, grad_conv_w, grad_conv_b, grad_dt_bias, grad_a_...]
    psum x0 -> x1, waiting for transfers between devices: none -> 44.8 us  [body(): summed_small = lax.psum(partial, 'dp')]
    psum x1, blocking collectives: 41.9 us -> 13.2 us  [body(): lax.psum((grad_norm_gain, grad_conv_w, grad_conv_b, grad_dt_bias, grad_a_...]
    psum x0 -> x1, blocking collectives: none -> 27.7 us  [body(): summed_small = lax.psum(partial, 'dp')]
    unnamed x159 -> x135, local copies, waits for them, and re-layouts: 35 us -> 33.4 us
  transfers between devices with their start and end apart: 11 -> 12, of which waited for: 10 -> 10; matrix products, arithmetic and copies ran while one was open for 15% -> 22% of each run, Pallas kernels for 0% -> 0%
where the time goes in v1:
time: 1390 us; the launch traced here: 1380 us
  waiting for transfers between devices  688 us (49%)
  local copies, waits for them, and re-layouts  232 us (17%)
  matrix products  191 us (14%)
  other arithmetic  133 us (10%)
  blocking collectives  97.3 us (7%)
  starting transfers between devices  17 us (1%)
  between operations  16.7 us (1%)
    reduce_scatter x1, waiting for transfers between devices, body(): lax.psum_scatter(jnp.concatenate([in_part, lax.dot_general(grad_gathered,...  249 us
    all_to_all x1, waiting for transfers between devices, body(): lax.all_to_all(outgoing, 'tp', split_axis=2, concat_axis=0, tiled=True)  141 us
    dot_general x3, matrix products, span_pass(): output = jnp.einsum('tsh,shp->thp', mixing, values, precision=HIGHEST)  65.5 us
    all_to_all x1, waiting for transfers between devices, body(): lax.all_to_all(blocks, 'tp', split_axis=0, concat_axis=2, tiled=True)  61.8 us
    all_gather x2, waiting for transfers between devices, entering_2(): everything = jax.tree.map(lambda part: lax.all_gather(part, axis), array)  57.1 us
    all_to_all x1, blocking collectives, body(): lax.all_to_all(rounded, 'tp', split_axis=1, concat_axis=0, tiled=True)  50.2 us
    reduce_scatter x1, waiting for transfers between devices, body(): lax.psum_scatter(jnp.dot(by_heads, w_out, preferred_element_type=jnp.floa...  47 us
    psum x1, waiting for transfers between devices, body(): summed_small = lax.psum(partial, 'dp')  44.8 us
  transfers between devices with their start and end apart: 12, of which 10 were waited for; matrix products, arithmetic and copies ran while one was open for 22% of the time, Pallas kernels for 0%

profile of v1, /device:TPU:1, one launch (start us, length us, event | category | flops | bytes accessed | tf_op | source)
XLA Modules:
  0.0 1375.8 jit_solution(6411934169579836168)
XLA Ops:
  12.3 14.3 %concatenate.29 = bf16[2048,2128]{1,0:T(8,128)(2,1)} concatenate(bf16[2048,1024]{1,0:T(8,128)(2,1)} %param.24, bf16[2048,1024]{1,0:T(8,128)(2,1)} %param.25, bf16[2048,32]{1,0:T(8,128)(2,1)S(1)} %copy.171, bf16[2048,32]{1,0:T(8,128)(2,1)S(1)} %copy.172, bf16[2048,16]{1,0:T(8,128)(2,1)S(1)} %copy.173), dimensions={1} | concatenate | bytes 17432576 | tf_op jit(solution)/shard_map/concatenate | solution.py:114
  26.6 39.8 %all-gather.8.cloned.1.call-done = bf16[1024,2048]{1,0:T(8,128)(2,1)} async-done(((bf16[256,2048]{1,0:T(8,128)(2,1)}), bf16[1024,2048]{1,0:T(8,128)(2,1)}) %all-gather.8.cloned.1.call-update) | async-done | bytes 4194320 | tf_op jit(solution)/shard_map/all_gather | solution.py:115
  66.3 13.6 convolution_convert_fusion
  82.0 4.6 pad_slice_fusion
  86.6 6.4 copy.204
  93.1 6.4 copy.203
  100.4 5.6 pad_maximum_fusion.1
  106.0 5.0 all-to-all-start
  116.2 61.8 %all-to-all-done = bf16[4,259,2128]{2,1,0:T(8,128)(2,1)} async-done(((bf16[4,259,2128]{2,1,0:T(8,128)(2,1)}), bf16[4,259,2128]{2,1,0:T(8,128)(2,1)}, u32[]{:S(2)}, u32[]{:S(2)}) %all-to-all-start) | async-done | bytes 4409248 | tf_op jit(solution)/shard_map/all_to_all | solution.py:120
  178.0 8.2 copy.176
  186.2 5.1 slice_bitcast_fusion
  205.8 4.9 fusion.25
  215.3 5.8 copy.180
  221.5 6.9 fusion.78
  228.5 8.0 convolution_convert_fusion.1
  239.1 4.5 all-to-all-start.2
  244.0 43.3 %all-to-all-done.2 = bf16[4,256,1024]{1,2,0:T(8,128)(2,1)} async-done(((bf16[4,256,1024]{1,2,0:T(8,128)(2,1)}), bf16[4,256,1024]{1,2,0:T(8,128)(2,1)}, u32[]{:S(2)}, u32[]{:S(2)}) %all-to-all-start.2) | async-done | bytes 2097184 | tf_op jit(solution)/shard_map/all_to_all | solution.py:205
  291.2 6.3 all-gather.2
  298.8 6.2 fusion.92
  308.8 32.8 %all-gather.12.cloned.1.call-done = f32[256,64,128]{2,1,0:T(8,128)} async-done(((f32[64,64,128]{2,1,0:T(8,128)}), f32[256,64,128]{2,1,0:T(8,128)}) %all-gather.12.cloned.1.call-update) | async-done | bytes 8388624 | tf_op jit(solution)/shard_map/all_gather | solution.py:12
  341.7 8.5 while.31
  350.1 4.5 fusion.100
  354.7 23.6 %multiply_reduce_fusion.11 = (f32[256]{0:T(256)S(1)}, f32[256,64,64]{0,2,1:T(8,128)S(1)}, f32[256,64,64]{0,2,1:T(8,128)}) fusion(f32[256,64,64]{0,2,1:T(8,128)} %bitcast.311, f32[256,64,64]{0,2,1:T(8,128)S(1)} %bitcast.299, f32[64]{0:T(128)S(1)} %copy-done.61, f32[256,64,64]{0,2,1:T(8,128)S(1)} %fusion.100, f32[256,64,64]{0,2,1:T(8,128)} %fusion.92, ...), kind=kOutput, calls=%fused_computation.87 | convolution fusion | flops 3251633920 | bytes 25691392 | tf_op jit(solution)/shard_map/jvp(tsh,shp->thp)/dot_general | solution.py:44
  380.5 6.1 multiply_reduce_fusion.6
  388.5 5.6 fusion.53
  397.5 5.0 fusion.28
  402.5 4.5 concatenate.33
  407.0 7.6 copy.193
  414.6 8.8 fusion.84
  423.4 6.7 fusion.81
  430.1 26.3 %fusion.10 = (f32[256,64]{0,1:T(8,128)}, f32[256,64]{0,1:T(8,128)}, f32[256,64]{0,1:T(8,128)}, f32[256,256]{1,0:T(8,128)S(1)}) fusion(f32[256,64]{0,1:T(8,128)S(1)} %get-tuple-element.463, f32[256,256]{1,0:T(8,128)S(1)} %copy-done.22, f32[256,64]{0,1:T(8,128)S(1)} %bitcast_bitcast_fusion.1, pred[256,256]{1,0:T(8,128)(4,1)S(1)} %fusion.95, ...), kind=kOutput, calls=%fused_computation.18 | convolution fusion | flops 3275636736 | bytes 9306112 | tf_op jit(solution)/shard_map/transpose(jvp(tsh,shp->thp))/dot_general | solution.py:44
  457.7 24.2 %all-gather.14.cloned.1.call-done = f32[256,64,128]{2,1,0:T(8,128)} async-done(((f32[64,64,128]{2,1,0:T(8,128)}), f32[256,64,128]{2,1,0:T(8,128)}) %all-gather.14.cloned.1.call-update) | async-done | bytes 8388624 | tf_op jit(solution)/shard_map/all_gather | solution.py:12
  481.9 14.9 %while.32 = (s32[]{:T(128)}, f32[64,64,128]{2,1,0:T(8,128)}, s32[]{:T(128)}, f32[4,64]{1,0:T(4,128)S(1)}, f32[4,64,64,128]{3,2,1,0:T(8,128)}, /*index=5*/s32[]{:T(128)}, s32[]{:T(128)}, s32[]{:T(128)}, s32[]{:T(128)}) while((s32[]{:T(128)}, f32[64,64,128]{2,1,0:T(8,128)}, s32[]{:T(128)}, f32[4,64]{1,0:T(4,128)S(1)}, ...), condition=%wide.region_12.13_spmd.clone, body=%wide.region_11.12_spmd.clone.sunk | while | flops 2097160 | bytes 6292391 | solution.py:25
  496.8 9.9 fusion.87
  506.7 4.5 multiply_reduce_fusion.9
  514.1 15.6 %fusion.31 = f32[256,64,64]{0,2,1:T(8,128)} fusion(f32[256,64,64]{0,2,1:T(8,128)S(1)} %get-tuple-element.475, f32[256,64,64]{0,2,1:T(8,128)S(1)} %copy-done.7, f32[64]{0:T(128)S(1)} %copy-done.61, f32[256,64]{0,1:T(8,128)S(1)} %get-tuple-element.462, f32[256,64]{0,1:T(8,128)S(1)} %get-tuple-element.463, f32[256,256]{1,0:T(8,128)S(1)} %copy-done.23, ...), kind=kOutput, calls=%fused_computation.58 | convolution fusion | flops 3242196992 | bytes 13107456 | tf_op jit(solution)/shard_map/transpose(jvp(tsh,shp->thp))/dot_general | solution.py:44
  529.7 6.1 copy.185
  535.8 12.3 multiply_reduce_fusion.4
  554.0 7.2 pad_add_fusion
  566.2 4.7 slice.230
  570.9 6.1 reshape.445
  577.0 15.8 %concatenate.35 = f32[259,4,2128]{2,1,0:T(4,128)} concatenate(f32[259,4,1024]{2,1,0:T(4,128)} %copy.193, f32[259,4,1024]{2,1,0:T(4,128)} %reshape.445, f32[259,4,32]{2,1,0:T(4,128)S(1)} %copy.194, f32[259,4,32]{2,1,0:T(4,128)S(1)} %copy.195, f32[259,4,16]{2,1,0:T(4,128)S(1)} %copy.196), dimensions={2} | concatenate | bytes 17636864 | tf_op jit(solution)/shard_map/concatenate | solution.py:242
  592.8 11.4 reshape.454
  604.2 27.3 %copy.197 = f32[1,259,8512]{1,0,2:T(1,128)} copy(f32[1,259,8512]{2,1,0:T(8,128)} %reshape.454) | data formatting | bytes 17636864 | tf_op jit(solution)/shard_map/reshape | solution.py:242
  631.5 6.5 all-to-all-start.3
  640.2 140.7 %all-to-all-done.3 = f32[1,259,8512]{1,0,2:T(1,128)} async-done(((f32[1,259,8512]{1,0,2:T(1,128)}), f32[1,259,8512]{1,0,2:T(1,128)}, u32[]{:S(2)}, u32[]{:S(2)}) %all-to-all-start.3) | async-done | bytes 8818464 | tf_op jit(solution)/shard_map/all_to_all | solution.py:245
  780.9 11.9 copy.207
  792.8 7.0 slice.233
  803.2 6.6 add_select_fusion
  809.8 22.4 %scatter-add.4 = f32[4,256,2128]{1,2,0:T(8,128)} dynamic-update-slice(f32[4,256,2128]{1,2,0:T(8,128)} %copy-done.8, f32[3,3,2128]{1,2,0:T(8,128)} %add_select_fusion, s32[]{:T(128)} %bitcast.52, s32[]{:T(128)} %bitcast.53, s32[]{:T(128)} %constant.140.clone.1) | dynamic-update-slice | bytes 153220 | tf_op jit(solution)/shard_map/scatter-add | solution.py:247
  832.2 5.9 convert_element_type.125
  838.1 6.5 copy.200
  844.6 15.7 %fusion.148 = f32[1024,2048]{1,0:T(8,128)} fusion(bf16[1024,2128]{1,0:T(8,128)(2,1)} %bitcast.319, bf16[2048,2128]{1,0:T(8,128)(2,1)} %concatenate.29), kind=kOutput, calls=%fused_computation.237 | convolution fusion | flops 8925478912 | bytes 21463040 | tf_op jit(solution)/shard_map/dot_general | solution.py:250
  864.7 50.2 %all_to_all.62 = bf16[256,4,1024]{0,2,1:T(8,128)(2,1)} all-to-all(bf16[256,4,1024]{0,2,1:T(8,128)(2,1)S(1)} %fusion.48), channel_id=1, replica_groups=mesh['dp'=8,'tp'=4] {'tp'}, dimensions={1} | all-to-all | bytes 4194304 | tf_op jit(solution)/shard_map/all_to_all | solution.py:193
  917.9 9.2 fusion.147
  927.1 9.1 convolution_bitcast_fusion
  936.2 12.9 fusion.149
  949.1 16.2 %pad_maximum_fusion = f32[2048,3152]{0,1:T(8,128)} fusion(f32[2048,1024]{0,1:T(8,128)} %convolution_bitcast_fusion, f32[2048,2128]{0,1:T(8,128)S(1)} %fusion.149), kind=kLoop, calls=%fused_computation.6 | loop fusion | flops 6455296 | bytes 51642368 | tf_op jit(solution)/shard_map/concatenate | solution.py:264
  972.4 13.2 all-reduce.17
  985.6 27.7 %all-reduce.16 = (f32[2048]{0:T(1024)}, f32[4352]{0:T(1024)}, f32[64]{0:T(128)}, f32[64]{0:T(128)}, f32[64]{0:T(128)}, /*index=5*/f32[4096]{0:T(1024)}) all-reduce(f32[2048]{0:T(1024)S(1)} %get-tuple-element.431, f32[4352]{0:T(1024)S(1)} %get-tuple-element.432, ...), channel_id=1, replica_groups=mesh['dp'=8,'tp'=4] {'dp'}, use_global_device_ids=true, to_apply=%region_31.32 | all-reduce | flops 10688 | bytes 85504 | tf_op jit(solution)/shard_map/psum | solution.py:295
  1013.4 47.0 %reduce-scatter.4.cloned.1.call-done = f32[256,2048]{1,0:T(8,128)} async-done(((f32[1024,2048]{1,0:T(8,128)}), f32[256,2048]{1,0:T(8,128)}) %reduce-scatter.4.cloned.1.call-update) | async-done | bytes 2097168 | tf_op jit(solution)/shard_map/reduce_scatter | solution.py:194
  1060.4 4.6 fusion.65
  1065.0 249.1 %reduce-scatter.8.cloned.1.call-done = f32[256,3152]{0,1:T(8,128)} async-done(((f32[2048,3152]{0,1:T(8,128)}), f32[256,3152]{0,1:T(8,128)}) %reduce-scatter.8.cloned.1.call-update) | async-done | bytes 3227664 | tf_op jit(solution)/shard_map/reduce_scatter | solution.py:263
  1322.5 44.8 %all-reduce.23.cloned.1.call-done = f32[4352,4]{0,1:T(4,128)} async-done(((f32[4352,4]{0,1:T(4,128)}), f32[4352,4]{0,1:T(4,128)}) %all-reduce.23.cloned.1.call-update) | async-done | bytes 69648 | tf_op jit(solution)/shard_map/psum | solution.py:295
  (257 shorter events, 118.6 us)
Async XLA Ops:
  7.2 4.2 copy-start.27
  7.2 4.5 copy-start.28
  7.2 4.8 copy-start.33
  7.2 59.1 %all-gather.8.cloned.1.call-start = ((), (), s32[]{:S(2)}) async-start(), calls=%async_computation.7 | async-start | bytes 5242880 | tf_op jit(solution)/shard_map/all_gather | solution.py:115
  8.8 2.6 copy-start.51
  106.0 6.4 copy-start.62
  106.0 6.4 copy-start.60
  106.0 8.6 copy-start.32
  106.0 72.0 %all-to-all-start = ((bf16[4,259,2128]{2,1,0:T(8,128)(2,1)}), bf16[4,259,2128]{2,1,0:T(8,128)(2,1)}, u32[]{:S(2)}, u32[]{:S(2)}) async-start(bf16[4,259,2128]{2,1,0:T(8,128)(2,1)} %pad_maximum_fusion.1), calls=%async_computation | async-start | bytes 9191424 | tf_op jit(solution)/shard_map/all_to_all | solution.py:120
  111.0 117.5 %all-gather.10.cloned.1.call-start = ((), (), s32[]{:S(2)}) async-start(), calls=%async_computation.9 | async-start | bytes 5242880 | tf_op jit(solution)/shard_map/all_gather | solution.py:201
  111.8 229.9 %all-gather.12.cloned.1.call-start = ((), (), s32[]{:S(2)}) async-start(), calls=%async_computation.14 | async-start | bytes 10485760 | tf_op jit(solution)/shard_map/all_gather | solution.py:12
  112.4 80.9 %copy-start.54 = (f32[64]{0:T(128)}, f32[64]{0:T(128)S(1)}, u32[]{:S(2)}) copy-start(f32[64]{0:T(128)S(1)} %exp.58) | copy-start | bytes 772
  116.2 105.2 %copy-start.49 = (pred[256]{0:T(512)(128)(4,1)}, pred[256]{0:T(512)(128)(4,1)S(1)}, u32[]{:S(2)}) copy-start(pred[256]{0:T(512)(128)(4,1)S(1)} %get-tuple-element.465) | copy-start | bytes 772
  116.2 419.6 %copy-start.40 = (f32[256]{0:T(256)}, f32[256]{0:T(256)S(1)}, u32[]{:S(2)}) copy-start(f32[256]{0:T(256)S(1)} %get-tuple-element.466) | copy-start | bytes 3076
  116.2 419.6 %copy-start.41 = (f32[256]{0:T(256)}, f32[256]{0:T(256)S(1)}, u32[]{:S(2)}) copy-start(f32[256]{0:T(256)S(1)} %get-tuple-element.467) | copy-start | bytes 3076
  116.2 419.6 %copy-start.42 = (f32[256]{0:T(256)}, f32[256]{0:T(256)S(1)}, u32[]{:S(2)}) copy-start(f32[256]{0:T(256)S(1)} %get-tuple-element.468) | copy-start | bytes 3076
  186.2 7.2 copy-start.45
  193.3 28.0 %copy-start.19 = (bf16[256,4,16]{0,2,1:T(8,128)(2,1)}, bf16[256,4,16]{0,2,1:T(8,128)(2,1)S(1)}, u32[]{:S(2)}) copy-start(bf16[256,4,16]{0,2,1:T(8,128)(2,1)S(1)} %slice.224) | copy-start | bytes 98308
  205.8 4.9 copy-start
  221.3 7.1 copy-start.47
  236.5 7.3 copy-start.24
  239.1 48.2 %all-to-all-start.2 = ((bf16[4,256,1024]{1,2,0:T(8,128)(2,1)}), bf16[4,256,1024]{1,2,0:T(8,128)(2,1)}, u32[]{:S(2)}, u32[]{:S(2)}) async-start(bf16[4,256,1024]{1,2,0:T(8,128)(2,1)} %copy.184), calls=%async_computation.3 | async-start | bytes 4194304 | tf_op jit(solution)/shard_map/all_to_all | solution.py:205
  243.7 238.2 %all-gather.14.cloned.1.call-start = ((), (), s32[]{:S(2)}) async-start(), calls=%async_computation.15 | async-start | bytes 10485760 | tf_op jit(solution)/shard_map/all_gather | solution.py:12
  298.8 55.9 %copy-start.21 = (f32[256,256]{1,0:T(8,128)}, f32[256,256]{1,0:T(8,128)S(1)}, u32[]{:S(2)}) copy-start(f32[256,256]{1,0:T(8,128)S(1)} %fusion.106) | copy-start | bytes 786436
  350.1 4.5 copy-start.2
  350.1 4.5 copy-start.61
  354.6 23.6 %copy-start.16 = (f32[256,64,64]{0,2,1:T(8,128)}, f32[256,64,64]{0,2,1:T(8,128)S(1)}, u32[]{:S(2)}) copy-start(f32[256,64,64]{0,2,1:T(8,128)S(1)} %fusion.100) | copy-start | bytes 12582916
  354.7 23.6 %copy-start.11 = (f32[4,256,1024]{1,2,0:T(8,128)S(1)}, f32[4,256,1024]{1,2,0:T(8,128)}, u32[]{:S(2)}) copy-start(f32[4,256,1024]{1,2,0:T(8,128)} %convert_element_type.132) | copy-start | bytes 12582916
  378.3 19.2 %copy-start.37 = (f32[256]{0:T(256)}, f32[256]{0:T(256)S(1)}, u32[]{:S(2)}) copy-start(f32[256]{0:T(256)S(1)} %fusion.132) | copy-start | bytes 3076
  414.6 8.8 copy-start.6
  423.4 6.7 copy-start.3
  423.4 6.7 copy-start.22
  496.8 9.9 copy-start.1
  496.8 9.9 copy-start.4
  511.2 2.8 copy-start.7
  511.2 2.8 copy-start.23
  550.3 3.4 copy-start.10
  553.8 7.3 copy-start.20
  553.9 7.3 copy-start.46
  553.9 7.3 copy-start.48
  553.9 7.3 copy-start.50
  553.9 7.6 copy-start.57
  553.9 7.6 copy-start.58
  553.9 7.8 copy-start.34
  553.9 7.8 copy-start.35
  553.9 10.7 copy-start.36
  553.9 10.6 copy-start.53
  554.0 10.6 copy-start.55
  631.5 7.2 copy-start.59
  631.5 7.9 copy-start.30
  631.5 149.4 %all-to-all-start.3 = ((f32[1,259,8512]{1,0,2:T(1,128)}), f32[1,259,8512]{1,0,2:T(1,128)}, u32[]{:S(2)}, u32[]{:S(2)}) async-start(f32[1,259,8512]{1,0,2:T(1,128)} %copy.197), calls=%async_computation.4 | async-start | bytes 26148864 | tf_op jit(solution)/shard_map/all_to_all | solution.py:245
  638.0 328.2 %all-reduce.21.cloned.1.call-start = ((), (), s32[]{:S(2)}) async-start(), calls=%async_computation.12 | async-start | bytes 139264 | tf_op jit(solution)/shard_map/psum | solution.py:283
  640.1 330.0 %reduce-scatter.6.cloned.1.call-start = ((), (), s32[]{:S(2)}) async-start(), calls=%async_computation.10 | async-start | bytes 10485760 | tf_op jit(solution)/shard_map/reduce_scatter | solution.py:249
  799.8 3.4 copy-start.8
  860.3 200.1 %reduce-scatter.4.cloned.1.call-start = ((), (), s32[]{:S(2)}) async-start(), calls=%async_computation.8 | async-start | bytes 10485760 | tf_op jit(solution)/shard_map/reduce_scatter | solution.py:194
  927.1 387.0 %reduce-scatter.8.cloned.1.call-start = ((), (), s32[]{:S(2)}) async-start(), calls=%async_computation.11 | async-start | bytes 29048832 | tf_op jit(solution)/shard_map/reduce_scatter | solution.py:263
  965.3 4.8 copy-start.17
  965.3 4.8 copy-start.31
  965.3 4.8 copy-start.44
  965.3 7.1 copy-start.52
  965.3 7.1 copy-start.29
  965.4 7.1 copy-start.56
  965.4 95.0 %copy-start.18 = (bf16[256,2048]{1,0:T(8,128)(2,1)S(1)}, bf16[256,2048]{1,0:T(8,128)(2,1)}, u32[]{:S(2)}) copy-start(bf16[256,2048]{1,0:T(8,128)(2,1)} %param.37) | copy-start | bytes 3145732
  965.4 401.9 %all-reduce.23.cloned.1.call-start = ((), (), s32[]{:S(2)}) async-start(), calls=%async_computation.13 | async-start | bytes 139264 | tf_op jit(solution)/shard_map/psum | solution.py:295
  (12 other events, 19.9 us)
Sparse Core Ops, SparseCore 0:
  11.5 54.7 all-gather.7
  113.7 83.3 all-gather.9
  228.6 113.0 all-gather.11
  394.2 87.6 all-gather.13
  642.0 162.0 all-reduce.20
  860.4 109.6 reduce-scatter.5
  973.2 87.1 reduce-scatter.3
  1062.9 251.2 reduce-scatter.7
  1316.5 50.8 all-reduce.22
